TPU v7x, 32 devices: a whole 2x2x4 slice. The times are simulated.
32 devices in a mesh: groups: 2 (over y), seq: 4 (over z), head: 2 (over x), rep: 2 (over core).
Axes of the slice: x: 2, y: 2, z: 4, core: 2. Of those that a mesh axis runs over, the one named last changes fastest.
Arguments:
- document_query: bfloat16 [4096, 8192], P(('groups', 'seq', 'rep'), 'head'), parts along dimension 0, may hold values from -6 to 6
- document_key: bfloat16 [4096, 8192], P(('groups', 'seq', 'rep'), 'head'), parts along dimension 0, may hold values from -0.059814453 to 0.059814453
- document_value: bfloat16 [4096, 8192], P(('groups', 'seq', 'rep'), 'head'), parts along dimension 0, may hold values from -6 to 6
- document_decay: float32 [4096, 64], P(('groups', 'seq', 'rep'), 'head'), parts along dimension 0, may hold values from 0 to 1, as said below
- passage_query: bfloat16 [16, 256, 8192], P(('groups', 'seq', 'rep'), None, 'head'), parts along dimension 0, may hold values from -6 to 6
- passage_key: bfloat16 [16, 256, 8192], P(('groups', 'seq', 'rep'), None, 'head'), parts along dimension 0, may hold values from -0.059814453 to 0.059814453
- passage_value: bfloat16 [16, 256, 8192], P(('groups', 'seq', 'rep'), None, 'head'), parts along dimension 0, may hold values from -6 to 6
- passage_gate: bfloat16 [16, 256, 8192], P(('groups', 'seq', 'rep'), None, 'head'), parts along dimension 0, may hold values from -8 to 8
- passage_decay: float32 [16, 256, 64], P(('groups', 'seq', 'rep'), None, 'head'), parts along dimension 0, may hold values from 0 to 1, as said below
- passage_length: int32 [16], P(('groups', 'seq', 'rep')), parts along dimension 0, may hold values from 64 to 256, as said below
- norm_gain: float32 [8192], P('head'), may hold values from 0.1 to 1.9
Outputs:
- document_output: bfloat16 [4096, 8192], P(('groups', 'seq', 'rep'), 'head'), parts along dimension 0
- passage_output: bfloat16 [16, 256, 8192], P(('groups', 'seq', 'rep'), None, 'head'), parts along dimension 0
There are 2 independent parts, one for each index of `groups`. A program takes and returns all parts, laid end to end along the dimension named above; an argument that names none is the same for every part. Nothing has to cross between parts.
Inputs may be any that keep to these rules, and one draw needn't show every extreme that they name: `document_decay`: positive per-position log-decay rates. `passage_decay`: positive per-position log-decay rates. `passage_length`: a passage's valid tokens are its first ones.
All inputs are finite; a program needn't handle non-finite values.
Results may differ from a plain program's by a relative error of at most 0.0046.
Values sent between devices are 32-bit elements; how exact they have to be, the bound alone decides.
A program may use at most 128 MiB of HBM per device.

v0:
```python
import jax
import jax.numpy as jnp
from jax import lax
from jax.sharding import PartitionSpec as P

epsilon = 1e-05


def entering_2(value, axis, combine, identity, reverse):
    peers, place = (lax.axis_size(axis), lax.axis_index(axis))
    everything = jax.tree.map(lambda part: lax.all_gather(part, axis), value)
    start = jax.tree.map(
        lambda part, zero: jnp.broadcast_to(jnp.asarray(zero, part.dtype), part.shape),
        value,
        identity,
    )

    def hop(k, before):
        at = peers - 1 - k if reverse else k
        reached = at > place if reverse else at < place
        new = combine(before, jax.tree.map(lambda part: part[at], everything))
        return jax.tree.map(lambda a, b: jnp.where(reached, a, b), new, before)

    return lax.fori_loop(0, peers, hop, start)


def local_block(queries, keys_in, values_in, rates):
    length = queries.shape[0]
    cumulative = jnp.cumsum(rates, axis=0)
    scores = jnp.einsum("thd,shd->hts", queries, keys_in, preferred_element_type=jnp.float32)
    ordered = jnp.transpose(cumulative)
    spread = ordered[:, None, :] - ordered[:, :, None]
    causal = (
        lax.broadcasted_iota(jnp.int32, (length, length), 0)
        >= lax.broadcasted_iota(jnp.int32, (length, length), 1)
    )[None]
    weights = jnp.where(causal, scores * jnp.exp(jnp.where(causal, spread, 0.0)), 0.0).astype(
        jnp.bfloat16
    )
    intra_part = jnp.einsum("hts,shd->thd", weights, values_in, preferred_element_type=jnp.float32)
    return (intra_part, cumulative)


def carried(queries, cumulative, state_full):
    inter_part = jnp.einsum(
        "thd,hde->the", queries.astype(jnp.float32), state_full, precision=lax.Precision.HIGHEST
    )
    return inter_part * jnp.exp(-cumulative)[:, :, None]


def block_state(keys_in, values_in, cumulative):
    closing = cumulative[-1]
    scaled_key = (
        keys_in.astype(jnp.float32) * jnp.exp(cumulative - closing[None, :])[:, :, None]
    ).astype(jnp.bfloat16)
    state = jnp.einsum("shd,she->hde", scaled_key, values_in, preferred_element_type=jnp.float32)
    return (state, jnp.exp(-closing))


def chain_step(earlier, later):
    return (earlier[0] * later[0], later[0][:, None, None] * earlier[1] + later[1])


def multiply(earlier, later):
    return earlier * later


def local(
    document_query,
    document_key,
    document_value,
    document_decay,
    passage_query,
    passage_key,
    passage_value,
    passage_gate,
    passage_decay,
    passage_length,
    norm_gain,
):
    heads_here = document_decay.shape[1]
    head_dim = document_query.shape[1] // heads_here
    doc_rows = document_query.shape[0]
    passage_count = passage_query.shape[0]
    passage_rows = passage_query.shape[1]
    doc_queries = document_query.reshape(doc_rows, heads_here, head_dim)
    doc_keys = document_key.reshape(doc_rows, heads_here, head_dim)
    doc_values = document_value.reshape(doc_rows, heads_here, head_dim)
    intra_doc, cumulative = local_block(doc_queries, doc_keys, doc_values, document_decay)
    state_own, decay_own = block_state(doc_keys, doc_values, cumulative)
    decay_before, entering = entering_2(
        (decay_own, state_own),
        ("seq", "rep"),
        chain_step,
        (jnp.ones_like(decay_own), jnp.zeros_like(state_own)),
        False,
    )
    document_output = (intra_doc + carried(doc_queries, cumulative, entering)).astype(jnp.bfloat16)
    document_output = document_output.reshape(doc_rows, heads_here * head_dim)
    decay_after = entering_2(decay_own, ("seq", "rep"), multiply, jnp.ones_like(decay_own), True)
    memory = lax.psum(decay_after[:, None, None] * state_own, ("seq", "rep"))

    def readout(inputs):
        queries, keys_in, values_in, rates = inputs
        queries = queries.reshape(passage_rows, heads_here, head_dim)
        intra_part, running = local_block(
            queries,
            keys_in.reshape(passage_rows, heads_here, head_dim),
            values_in.reshape(passage_rows, heads_here, head_dim),
            rates,
        )
        attended = (intra_part + carried(queries, running, memory)).reshape(
            passage_rows, heads_here * head_dim
        )
        return (attended, jnp.sum(attended * attended, axis=1))

    attended, squares = lax.map(readout, (passage_query, passage_key, passage_value, passage_decay))
    totals = lax.psum(squares, "head")
    features_all = attended.shape[-1] * lax.axis_size("head")
    scaling = lax.rsqrt(totals / features_all + epsilon)
    normed = (
        attended
        * scaling[:, :, None]
        * norm_gain[None, None, :]
        * jax.nn.sigmoid(passage_gate.astype(jnp.float32))
    )
    inside = (
        lax.broadcasted_iota(jnp.int32, (passage_count, passage_rows), 1) < passage_length[:, None]
    )
    passage_output = jnp.where(inside[:, :, None], normed, 0.0).astype(jnp.bfloat16)
    return (document_output, passage_output)


def solution(mesh):
    in_specs = (
        P(("groups", "seq", "rep"), "head"),
        P(("groups", "seq", "rep"), "head"),
        P(("groups", "seq", "rep"), "head"),
        P(("groups", "seq", "rep"), "head"),
        P(("groups", "seq", "rep"), None, "head"),
        P(("groups", "seq", "rep"), None, "head"),
        P(("groups", "seq", "rep"), None, "head"),
        P(("groups", "seq", "rep"), None, "head"),
        P(("groups", "seq", "rep"), None, "head"),
        P(("groups", "seq", "rep")),
        P("head"),
    )
    out_specs = (P(("groups", "seq", "rep"), "head"), P(("groups", "seq", "rep"), None, "head"))
    return jax.shard_map(local, mesh=mesh, in_specs=in_specs, out_specs=out_specs, check_vma=False)
```

profile of v0, /device:TPU:0, one launch (start us, length us, event | category | flops | bytes accessed | tf_op | source)
XLA Modules:
  0.0 281.8 jit_solution(3076644146216741903)
XLA Ops:
  7.2 0.9 copy_bitcast_fusion.3
  8.1 0.6 reduce-window.14
  8.7 0.2 slice_reduce_fusion.1
  9.0 0.2 slice_reduce_fusion.2
  9.3 13.5 %all-gather.1 = f32[8,1,32]{2,1,0:T(1,128)S(1)} all-gather(f32[1,1,32]{2,1,0:T(1,128)S(1)} %bitcast.131), channel_id=1, replica_groups=mesh['groups'=2,'seq'=4,'head'=2,'rep'=2] {'seq','rep'}, dimensions={0}, use_global_device_ids=true | all-gather | bytes 1152 | tf_op jit(solution)/shard_map/all_gather | solution.py:11
  22.8 0.3 while.36
  23.1 4.1 %copy.82 = bf16[256,4096]{0,1:T(8,128)(2,1)} copy(bf16[256,4096]{1,0:T(8,128)(2,1)} %param.16) | data formatting | bytes 4194304 | tf_op jit(solution)/shard_map/reshape | solution.py:87
  27.1 4.4 %broadcast_multiply_fusion = (f32[32,128,128]{2,1,0:T(8,128)}, f32[32,128,128]{2,1,0:T(8,128)}) fusion(f32[32]{0:T(128)S(1)} %get-tuple-element.231, bf16[256,32,128]{0,2,1:T(8,128)(2,1)} %bitcast.121, f32[256,32]{0,1:T(8,128)S(1)} %get-tuple-element.294, bf16[256,4096]{1,0:T(8,128)(2,1)S(1)} %copy-done), kind=kOutput, calls=%fused_computation.40 | convolution fusion | flops 272105472 | bytes 8421504 | tf_op jit(solution)/shard_map/shd,she->hde/dot_general | solution.py:56
  31.6 0.7 all-gather.4.cloned.1.call-update
  32.3 0.6 reduce-window.16
  33.1 3.4 %copy.89 = bf16[32,8,32,128]{3,2,1,0:T(8,128)(2,1)} copy(bf16[32,8,32,128]{3,1,2,0:T(8,128)(2,1)} %bitcast.124) | data formatting | bytes 4194304
  36.5 4.1 %copy.81 = bf16[1,256,4096]{1,2,0:T(8,128)(2,1)} copy(bf16[1,256,4096]{2,1,0:T(8,128)(2,1)} %param.21) | data formatting | bytes 4194304 | tf_op jit(solution)/shard_map/while/body/eval_jaxpr/reshape | solution.py:109
  40.6 3.5 %copy.90 = bf16[32,8,32,128]{3,2,1,0:T(8,128)(2,1)} copy(bf16[32,8,32,128]{3,1,2,0:T(8,128)(2,1)} %bitcast.125) | data formatting | bytes 4194304
  45.0 6.4 %fusion.1 = f32[32,256,128]{1,2,0:T(8,128)} fusion(f32[32,256]{1,0:T(8,128)S(1)} %get-tuple-element.296, pred[256,256]{1,0:T(8,128)(4,1)S(1)} %iota_compare_fusion, bf16[256,32,128]{0,2,1:T(8,128)(2,1)} %bitcast.122, bf16[256,4096]{1,0:T(8,128)(2,1)S(1)} %copy-done, bf16[256,4096]{1,0:T(8,128)(2,1)} %param.15), kind=kOutput, calls=%fused_computation.7 | convolution fusion | flops 1084227584 | bytes 10584064 | tf_op jit(solution)/shard_map/hts,shd->thd/dot_general | solution.py:40
  51.3 7.3 %fusion.2 = f32[32,256,128]{1,2,0:T(8,128)} fusion(bf16[256,32,128]{0,2,1:T(8,128)(2,1)} %bitcast.126, f32[32,256]{1,0:T(8,128)S(1)} %copy_bitcast_fusion, pred[256,256]{1,0:T(8,128)(4,1)S(1)} %iota_compare_fusion, bf16[256,32,128]{2,1,0:T(8,128)(2,1)} %bitcast.127, bf16[256,32,128]{2,1,0:T(8,128)(2,1)} %bitcast.118), kind=kOutput, calls=%fused_computation.8 | convolution fusion | flops 1084227584 | bytes 10584064 | tf_op jit(solution)/shard_map/while/body/eval_jaxpr/hts,shd->thd/dot_general | solution.py:40
  58.7 36.5 %all-reduce.2.cloned.1.call-done = f32[32,128,128]{2,1,0:T(8,128)} async-done(((f32[32,128,128]{2,1,0:T(8,128)}), f32[32,128,128]{2,1,0:T(8,128)}) %all-reduce.2.cloned.1.call-update) | async-done | bytes 2097168 | tf_op jit(solution)/shard_map/psum | solution.py:101
  95.1 7.8 %multiply_reduce_fusion = (f32[256]{0:T(256)S(1)}, f32[256,32,128]{0,2,1:T(8,128)}) fusion(f32[256,32]{0,1:T(8,128)S(1)} %exponential_bitcast_fusion, f32[32,128,128]{2,1,0:T(8,128)} %all-reduce.2.cloned.1.call-done, bf16[256,32,128]{2,1,0:T(8,128)(2,1)S(1)} %bitcast.119, f32[32,256,128]{1,2,0:T(8,128)} %fusion.2), kind=kOutput, calls=%fused_computation.15 | convolution fusion | flops 1614806784 | bytes 12616704 | tf_op jit(solution)/shard_map/while/body/eval_jaxpr/thd,hde->the/dot_general | solution.py:45
  102.9 6.1 %copy.77 = f32[1,256,4096]{2,1,0:T(8,128)} copy(f32[1,256,4096]{1,2,0:T(8,128)} %bitcast.117) | data formatting | bytes 8388608 | tf_op jit(solution)/shard_map/while/body/jit(dynamic_update_index_in_dim)/broadcast_in_dim | solution.py:117
  108.9 5.1 %psum.15 = f32[1,256]{1,0:T(1,128)S(1)} all-reduce(f32[1,256]{1,0:T(1,128)S(1)} %bitcast.129), channel_id=1, replica_groups=mesh['groups'=2,'seq'=4,'head'=2,'rep'=2] {'head'}, use_global_device_ids=true, to_apply=%region_10.11 | all-reduce | flops 256 | bytes 2048 | tf_op jit(solution)/shard_map/psum | solution.py:118
  114.0 5.9 %select_convert_fusion.4 = bf16[1,256,4096]{2,1,0:T(8,128)(2,1)} fusion(bf16[1,256,4096]{2,1,0:T(8,128)(2,1)} %param.22, f32[1,256,4096]{2,1,0:T(8,128)} %copy.77, f32[4096]{0:T(1024)S(1)} %copy-done.5, f32[256]{0:T(256)S(1)} %bitcast.130, pred[256]{0:T(512)(128)(4,1)S(1)} %iota_compare_fusion.1), kind=kLoop, calls=%fused_computation.14 | loop fusion | flops 9437184 | bytes 8406272 | tf_op jit(solution)/shard_map/convert_element_type | solution.py:130
  119.9 127.5 %all-gather.4.cloned.1.call-done = f32[256,128,128]{2,1,0:T(8,128)} async-done(((f32[32,128,128]{2,1,0:T(8,128)}), f32[256,128,128]{2,1,0:T(8,128)}) %all-gather.4.cloned.1.call-update) | async-done | bytes 16777232 | tf_op jit(solution)/shard_map/all_gather | solution.py:11
  247.4 17.0 %while.35 = (s32[]{:T(128)}, f32[32,128,128]{2,1,0:T(8,128)S(1)}, s32[]{:T(128)}, f32[8,32]{1,0:T(8,128)S(1)}, f32[8,32,128,128]{3,2,1,0:T(8,128)}, /*index=5*/s32[]{:T(128)}, s32[]{:T(128)}) while((s32[]{:T(128)}, f32[32,128,128]{2,1,0:T(8,128)S(1)}, s32[]{:T(128)}, f32[8,32]{1,0:T(8,128)S(1)}, f32[8,32,128,128]{3,2,1,0:T(8,128)}, ...), condition=%wide.region_3.4_spmd.clone, body=%wide.region_2.3_spmd.clone.sunk | while | flops 2097156 | bytes 6291945 | solution.py:24
  247.4 2.1 fusion.49
  249.6 2.1 fusion.49
  251.7 2.1 fusion.49
  253.8 2.1 fusion.49
  256.0 2.1 fusion.49
  258.1 2.1 fusion.49
  260.2 2.1 fusion.49
  262.4 2.1 fusion.49
  264.5 6.3 %fusion.5 = bf16[256,32,128]{0,2,1:T(8,128)(2,1)} fusion(f32[32,256,128]{1,2,0:T(8,128)} %fusion.1, f32[32,128,128]{2,1,0:T(8,128)S(1)} %get-tuple-element.230, f32[256,32]{0,1:T(8,128)S(1)} %get-tuple-element.293, bf16[256,4096]{1,0:T(8,128)(2,1)} %param.15), kind=kOutput, calls=%fused_computation.13 | convolution fusion | flops 1613758464 | bytes 10518528 | tf_op jit(solution)/shard_map/thd,hde->the/dot_general | solution.py:45
  270.8 4.2 %copy.78 = bf16[256,4096]{1,0:T(8,128)(2,1)} copy(bf16[256,4096]{0,1:T(8,128)(2,1)} %bitcast.120) | data formatting | bytes 4194304
  (46 shorter events, 0.9 us)
Async XLA Ops:
  7.2 20.0 %copy-start = (bf16[256,4096]{1,0:T(8,128)(2,1)S(1)}, bf16[256,4096]{1,0:T(8,128)(2,1)}, u32[]{:S(2)}) copy-start(bf16[256,4096]{1,0:T(8,128)(2,1)} %param.17) | copy-start | bytes 6291460
  7.2 87.9 %all-reduce.2.cloned.1.call-start = ((), (), s32[]{:S(2)}) async-start(), calls=%async_computation | async-start | bytes 4194304 | tf_op jit(solution)/shard_map/psum | solution.py:101
  31.5 0.8 copy-start.4
  31.6 215.9 %all-gather.4.cloned.1.call-start = ((), (), s32[]{:S(2)}) async-start(), calls=%async_computation.1 | async-start | bytes 18874368 | tf_op jit(solution)/shard_map/all_gather | solution.py:11
  51.3 43.8 %copy-start.3 = (bf16[32,8,32,128]{3,2,1,0:T(8,128)(2,1)S(1)}, bf16[32,8,32,128]{3,2,1,0:T(8,128)(2,1)}, u32[]{:S(2)}) copy-start(bf16[32,8,32,128]{3,2,1,0:T(8,128)(2,1)} %copy.89) | copy-start | bytes 6291460
  102.9 11.2 %copy-start.5 = (f32[4096]{0:T(1024)S(1)}, f32[4096]{0:T(1024)}, u32[]{:S(2)}) copy-start(f32[4096]{0:T(1024)} %param.25) | copy-start | bytes 49156
  114.0 133.4 %copy-start.2 = (f32[32,128,128]{2,1,0:T(8,128)S(1)}, f32[32,128,128]{2,1,0:T(8,128)}, u32[]{:S(2)}) copy-start(f32[32,128,128]{2,1,0:T(8,128)} %custom-call) | copy-start | bytes 6291460
  270.8 4.2 %copy-start.1 = (bf16[256,4096]{1,0:T(8,128)(2,1)S(1)}, bf16[256,4096]{1,0:T(8,128)(2,1)}, u32[]{:S(2)}) copy-start(bf16[256,4096]{1,0:T(8,128)(2,1)} %param.17) | copy-start | bytes 6291460
Sparse Core Ops, SparseCore 0:
  31.7 63.3 all-reduce.1
  96.7 150.6 all-gather.3
where the time goes:
time: 283 us; the launch traced here: 282 us
  waiting for transfers between devices  165 us (58%)
  matrix products  32.1 us (11%)
  local copies, waits for them, and re-layouts  26.6 us (9%)
  other arithmetic  24.6 us (9%)
  blocking collectives  18.6 us (7%)
  between operations  14.8 us (5%)
    all_gather x1, waiting for transfers between devices, entering_2(): everything = jax.tree.map(lambda part: lax.all_gather(part, axis), value)  128 us
    psum x1, waiting for transfers between devices, local(): memory = lax.psum(decay_after[:, None, None] * state_own, ('seq', 'rep'))  36.5 us
    select_n x16, other arithmetic, hop(): return jax.tree.map(lambda a, b: jnp.where(reached, a, b), new, before)  16.9 us
    dot_general x2, matrix products, carried(): jnp.einsum('thd,hde->the', queries.astype(jnp.float32), state_full, preci...  14 us
    dot_general x2, matrix products, local_block(): jnp.einsum('hts,shd->thd', weights, values_in, preferred_element_type=jnp...  13.7 us
    all_gather x1, blocking collectives, entering_2(): everything = jax.tree.map(lambda part: lax.all_gather(part, axis), value)  13.5 us
    unnamed x15, local copies, waits for them, and re-layouts  11.1 us
    broadcast_in_dim x1, local copies, waits for them, and re-layouts, local(): lax.map(readout, (passage_query, passage_key, passage_value, passage_decay))  6.07 us
  transfers between devices with their start and end apart: 2, of which 2 were waited for; matrix products, arithmetic and copies ran while one was open for 16% of the time, Pallas kernels for 0%

commit v1 on v0

--- a/solution.py
+++ b/solution.py
@@ -98,7 +98,7 @@
     document_output = (intra_doc + carried(doc_queries, cumulative, entering)).astype(jnp.bfloat16)
     document_output = document_output.reshape(doc_rows, heads_here * head_dim)
     decay_after = entering_2(decay_own, ("seq", "rep"), multiply, jnp.ones_like(decay_own), True)
-    memory = lax.psum(decay_after[:, None, None] * state_own, ("seq", "rep"))
+    memory = jnp.sum(lax.all_gather(decay_after[:, None, None] * state_own, ("seq", "rep")), axis=0)
 
     def readout(inputs):
         queries, keys_in, values_in, rates = inputs

time: 283 us -> 373 us (1.32)
  waiting for transfers between devices: 165 us -> 244 us
  other arithmetic: 24.6 us -> 33.7 us
    all_gather x0 -> x1, waiting for transfers between devices: none -> 122 us  [local(): lax.all_gather(decay_after[:, None, None] * state_own, ('seq', 'rep'))]
    psum x1 -> x0, waiting for transfers between devices: 36.5 us -> none  [local(): memory = lax.psum(decay_after[:, None, None] * state_own, ('seq', 'rep'))]
    reduce_sum x0 -> x1, other arithmetic: none -> 9.21 us  [local(): jnp.sum(lax.all_gather(decay_after[:, None, None] * state_own, ('seq', 'r...]
    all_gather x1, waiting for transfers between devices: 128 us -> 122 us  [entering_2(): everything = jax.tree.map(lambda part: lax.all_gather(part, axis), value)]
  transfers between devices with their start and end apart: 2 -> 2, of which waited for: 2 -> 2; matrix products, arithmetic and copies ran while one was open for 16% -> 14% of each run, Pallas kernels for 0% -> 0%
where the time goes in v1:
time: 373 us; the launch traced here: 372 us
  waiting for transfers between devices  244 us (65%)
  other arithmetic  33.7 us (9%)
  matrix products  33 us (9%)
  local copies, waits for them, and re-layouts  27.1 us (7%)
  blocking collectives  18.6 us (5%)
  between operations  14.8 us (4%)
    all_gather x1, waiting for transfers between devices, local(): lax.all_gather(decay_after[:, None, None] * state_own, ('seq', 'rep'))  122 us
    all_gather x1, waiting for transfers between devices, entering_2(): everything = jax.tree.map(lambda part: lax.all_gather(part, axis), value)  122 us
    select_n x16, other arithmetic, hop(): return jax.tree.map(lambda a, b: jnp.where(reached, a, b), new, before)  16.9 us
    dot_general x2, matrix products, carried(): jnp.einsum('thd,hde->the', queries.astype(jnp.float32), state_full, preci...  15.2 us
    dot_general x2, matrix products, local_block(): jnp.einsum('hts,shd->thd', weights, values_in, preferred_element_type=jnp...  13.5 us
    all_gather x1, blocking collectives, entering_2(): everything = jax.tree.map(lambda part: lax.all_gather(part, axis), value)  13.5 us
    unnamed x15, local copies, waits for them, and re-layouts  11.5 us
    reduce_sum x1, other arithmetic, local(): jnp.sum(lax.all_gather(decay_after[:, None, None] * state_own, ('seq', 'r...  9.21 us
  transfers between devices with their start and end apart: 2, of which 2 were waited for; matrix products, arithmetic and copies ran while one was open for 14% of the time, Pallas kernels for 0%

profile of v1, /device:TPU:0, one launch (start us, length us, event | category | flops | bytes accessed | tf_op | source)
XLA Modules:
  0.0 371.8 jit_solution(14747369189208727173)
XLA Ops:
  7.2 0.9 copy_bitcast_fusion.3
  8.1 0.6 reduce-window.14
  9.0 0.2 slice_reduce_fusion.2
  9.3 13.5 %all-gather.2 = f32[8,1,32]{2,1,0:T(1,128)S(1)} all-gather(f32[1,1,32]{2,1,0:T(1,128)S(1)} %bitcast.133), channel_id=1, replica_groups=mesh['groups'=2,'seq'=4,'head'=2,'rep'=2] {'seq','rep'}, dimensions={0}, use_global_device_ids=true | all-gather | bytes 1152 | tf_op jit(solution)/shard_map/all_gather | solution.py:11
  22.8 0.3 while.36
  23.1 4.1 %copy.79 = bf16[256,4096]{0,1:T(8,128)(2,1)} copy(bf16[256,4096]{1,0:T(8,128)(2,1)} %param.16) | data formatting | bytes 4194304 | tf_op jit(solution)/shard_map/reshape | solution.py:87
  27.1 4.3 %broadcast_multiply_fusion = (f32[32,128,128]{2,1,0:T(8,128)}, f32[32,128,128]{2,1,0:T(8,128)}) fusion(f32[32]{0:T(128)S(1)} %get-tuple-element.231, bf16[256,32,128]{0,2,1:T(8,128)(2,1)} %bitcast.123, f32[256,32]{0,1:T(8,128)S(1)} %get-tuple-element.294, bf16[256,4096]{1,0:T(8,128)(2,1)S(1)} %copy-done), kind=kOutput, calls=%fused_computation.40 | convolution fusion | flops 272105472 | bytes 8421504 | tf_op jit(solution)/shard_map/shd,she->hde/dot_general | solution.py:56
  31.5 0.7 all-gather.6.cloned.1.call-update
  32.2 0.6 reduce-window.16
  33.0 3.4 copy.86
  36.5 4.3 %copy.78 = bf16[1,256,4096]{1,2,0:T(8,128)(2,1)} copy(bf16[1,256,4096]{2,1,0:T(8,128)(2,1)} %param.21) | data formatting | bytes 4194304 | tf_op jit(solution)/shard_map/while/body/eval_jaxpr/reshape | solution.py:109
  40.7 4.0 %copy.87 = bf16[32,8,32,128]{3,2,1,0:T(8,128)(2,1)} copy(bf16[32,8,32,128]{3,1,2,0:T(8,128)(2,1)} %bitcast.127) | data formatting | bytes 4194304
  45.6 6.4 %fusion.1 = f32[32,256,128]{1,2,0:T(8,128)} fusion(f32[32,256]{1,0:T(8,128)S(1)} %get-tuple-element.296, pred[256,256]{1,0:T(8,128)(4,1)S(1)} %iota_compare_fusion, bf16[256,32,128]{0,2,1:T(8,128)(2,1)} %bitcast.124, bf16[256,4096]{1,0:T(8,128)(2,1)S(1)} %copy-done, bf16[256,4096]{1,0:T(8,128)(2,1)} %param.15), kind=kOutput, calls=%fused_computation.7 | convolution fusion | flops 1084227584 | bytes 10584064 | tf_op jit(solution)/shard_map/hts,shd->thd/dot_general | solution.py:40
  52.0 7.1 %fusion.2 = f32[32,256,128]{1,2,0:T(8,128)} fusion(bf16[256,32,128]{0,2,1:T(8,128)(2,1)} %bitcast.128, f32[32,256]{1,0:T(8,128)S(1)} %copy_bitcast_fusion, pred[256,256]{1,0:T(8,128)(4,1)S(1)} %iota_compare_fusion, bf16[256,32,128]{2,1,0:T(8,128)(2,1)} %bitcast.129, bf16[256,32,128]{2,1,0:T(8,128)(2,1)} %bitcast.120), kind=kOutput, calls=%fused_computation.8 | convolution fusion | flops 1084227584 | bytes 10584064 | tf_op jit(solution)/shard_map/while/body/eval_jaxpr/hts,shd->thd/dot_general | solution.py:40
  59.1 121.8 %all-gather.8.cloned.1.call-done = f32[256,128,128]{2,1,0:T(8,128)} async-done(((f32[32,128,128]{2,1,0:T(8,128)}), f32[256,128,128]{2,1,0:T(8,128)}) %all-gather.8.cloned.1.call-update) | async-done | bytes 16777232 | tf_op jit(solution)/shard_map/all_gather | solution.py:101
  180.9 9.2 %reduce_sum.19 = f32[32,128,128]{2,1,0:T(8,128)} reduce(f32[8,32,128,128]{3,2,1,0:T(8,128)} %bitcast.119, f32[]{:T(128)} %constant.101.clone.1), dimensions={0}, to_apply=%region_8.9 | reduce | flops 3670016 | bytes 18874372 | tf_op jit(solution)/shard_map/reduce_sum | solution.py:101
  190.1 9.0 %multiply_reduce_fusion = (f32[256]{0:T(256)S(1)}, f32[256,32,128]{0,2,1:T(8,128)}) fusion(f32[256,32]{0,1:T(8,128)S(1)} %exponential_bitcast_fusion, f32[32,128,128]{2,1,0:T(8,128)} %reduce_sum.19, bf16[256,32,128]{2,1,0:T(8,128)(2,1)S(1)} %bitcast.121, f32[32,256,128]{1,2,0:T(8,128)} %fusion.2), kind=kOutput, calls=%fused_computation.15 | convolution fusion | flops 1614806784 | bytes 12616704 | tf_op jit(solution)/shard_map/while/body/eval_jaxpr/thd,hde->the/dot_general | solution.py:45
  199.1 5.9 %copy.74 = f32[1,256,4096]{2,1,0:T(8,128)} copy(f32[1,256,4096]{1,2,0:T(8,128)} %bitcast.118) | data formatting | bytes 8388608 | tf_op jit(solution)/shard_map/while/body/jit(dynamic_update_index_in_dim)/broadcast_in_dim | solution.py:117
  205.0 5.1 %psum.7 = f32[1,256]{1,0:T(1,128)S(1)} all-reduce(f32[1,256]{1,0:T(1,128)S(1)} %bitcast.132), channel_id=1, replica_groups=mesh['groups'=2,'seq'=4,'head'=2,'rep'=2] {'head'}, use_global_device_ids=true, to_apply=%region_10.11 | all-reduce | flops 256 | bytes 2048 | tf_op jit(solution)/shard_map/psum | solution.py:118
  210.1 121.7 %all-gather.6.cloned.1.call-done = f32[256,128,128]{2,1,0:T(8,128)} async-done(((f32[32,128,128]{2,1,0:T(8,128)}), f32[256,128,128]{2,1,0:T(8,128)}) %all-gather.6.cloned.1.call-update) | async-done | bytes 16777232 | tf_op jit(solution)/shard_map/all_gather | solution.py:11
  331.8 17.0 %while.35 = (s32[]{:T(128)}, f32[32,128,128]{2,1,0:T(8,128)S(1)}, s32[]{:T(128)}, f32[8,32]{1,0:T(8,128)S(1)}, f32[8,32,128,128]{3,2,1,0:T(8,128)}, /*index=5*/s32[]{:T(128)}, s32[]{:T(128)}) while((s32[]{:T(128)}, f32[32,128,128]{2,1,0:T(8,128)S(1)}, s32[]{:T(128)}, f32[8,32]{1,0:T(8,128)S(1)}, f32[8,32,128,128]{3,2,1,0:T(8,128)}, ...), condition=%wide.region_3.4_spmd.clone, body=%wide.region_2.3_spmd.clone.sunk | while | flops 2097156 | bytes 6291945 | solution.py:24
  331.8 2.1 fusion.49
  334.0 2.1 fusion.49
  336.1 2.1 fusion.49
  338.2 2.1 fusion.49
  340.4 2.1 fusion.49
  342.5 2.1 fusion.49
  344.6 2.1 fusion.49
  346.8 2.1 fusion.49
  348.9 6.3 %fusion.5 = bf16[256,32,128]{0,2,1:T(8,128)(2,1)} fusion(f32[32,256,128]{1,2,0:T(8,128)} %fusion.1, f32[32,128,128]{2,1,0:T(8,128)S(1)} %get-tuple-element.230, f32[256,32]{0,1:T(8,128)S(1)} %get-tuple-element.293, bf16[256,4096]{1,0:T(8,128)(2,1)} %param.15), kind=kOutput, calls=%fused_computation.13 | convolution fusion | flops 1613758464 | bytes 10518528 | tf_op jit(solution)/shard_map/thd,hde->the/dot_general | solution.py:45
  355.1 4.1 %copy.75 = bf16[256,4096]{1,0:T(8,128)(2,1)} copy(bf16[256,4096]{0,1:T(8,128)(2,1)} %bitcast.122) | data formatting | bytes 4194304
  359.2 5.8 %select_convert_fusion.4 = bf16[1,256,4096]{2,1,0:T(8,128)(2,1)} fusion(bf16[1,256,4096]{2,1,0:T(8,128)(2,1)} %param.22, f32[1,256,4096]{2,1,0:T(8,128)} %copy.74, f32[4096]{0:T(1024)S(1)} %copy-done.5, f32[256]{0:T(256)S(1)} %bitcast.131, pred[256]{0:T(512)(128)(4,1)S(1)} %iota_compare_fusion.1), kind=kLoop, calls=%fused_computation.14 | loop fusion | flops 9437184 | bytes 8406272 | tf_op jit(solution)/shard_map/convert_element_type | solution.py:130
  (47 shorter events, 1.1 us)
Async XLA Ops:
  7.2 20.0 %copy-start = (bf16[256,4096]{1,0:T(8,128)(2,1)S(1)}, bf16[256,4096]{1,0:T(8,128)(2,1)}, u32[]{:S(2)}) copy-start(bf16[256,4096]{1,0:T(8,128)(2,1)} %param.17) | copy-start | bytes 6291460
  7.2 173.7 %all-gather.8.cloned.1.call-start = ((), (), s32[]{:S(2)}) async-start(), calls=%async_computation.1 | async-start | bytes 18874368 | tf_op jit(solution)/shard_map/all_gather | solution.py:101
  31.4 0.8 copy-start.4
  31.4 300.4 %all-gather.6.cloned.1.call-start = ((), (), s32[]{:S(2)}) async-start(), calls=%async_computation | async-start | bytes 18874368 | tf_op jit(solution)/shard_map/all_gather | solution.py:11
  180.9 9.2 %copy-start.3 = (bf16[32,8,32,128]{3,2,1,0:T(8,128)(2,1)S(1)}, bf16[32,8,32,128]{3,2,1,0:T(8,128)(2,1)}, u32[]{:S(2)}) copy-start(bf16[32,8,32,128]{3,2,1,0:T(8,128)(2,1)} %copy.86) | copy-start | bytes 6291460
  199.1 132.7 %copy-start.2 = (f32[32,128,128]{2,1,0:T(8,128)S(1)}, f32[32,128,128]{2,1,0:T(8,128)}, u32[]{:S(2)}) copy-start(f32[32,128,128]{2,1,0:T(8,128)} %custom-call) | copy-start | bytes 6291460
  355.1 4.1 %copy-start.5 = (f32[4096]{0:T(1024)S(1)}, f32[4096]{0:T(1024)}, u32[]{:S(2)}) copy-start(f32[4096]{0:T(1024)} %param.25) | copy-start | bytes 49156
  359.2 5.8 %copy-start.1 = (bf16[256,4096]{1,0:T(8,128)(2,1)S(1)}, bf16[256,4096]{1,0:T(8,128)(2,1)}, u32[]{:S(2)}) copy-start(bf16[256,4096]{1,0:T(8,128)(2,1)} %param.17) | copy-start | bytes 6291460
Sparse Core Ops, SparseCore 0:
  31.6 149.3 all-gather.7
  182.5 149.2 all-gather.5
